TPU v7x, 256 devices: a whole 4x4x8 slice. The times are simulated.
256 devices in a mesh: dp: 32 (over y, z_hi, core), ctx: 8 (over z_lo, x).
Axes of the slice: x: 4, y: 4, z: 8 (z_hi: 4, z_lo: 2; z = z_hi * 2 + z_lo), core: 2. Of those that a mesh axis runs over, the one named last changes fastest.
Arguments:
- q_feat: bfloat16 [16384, 4096], P('ctx', 'dp'), may hold values from -6 to 6
- k_feat: bfloat16 [16384, 4096], P('ctx', 'dp'), may hold values from -6 to 6
- v_feat: bfloat16 [16384, 4096], P('ctx', 'dp'), may hold values from -6 to 6
- short_taps: float32 [3, 4096], P(None, 'dp'), may hold values from -3 to 3
- skip_bias: float32 [4096], P('dp'), may hold values from -4 to 4
- freqs: float32 [32], replicated, may hold values from 1 to 8192
- phases: float32 [32], replicated, may hold values from -3.140625 to 3.140625
- w_first: float32 [32, 64], replicated, may hold values from -1 to 1
- b_first: float32 [64], replicated, may hold values from -4 to 4
- w_second: float32 [64, 64], replicated, may hold values from -0.75 to 0.75
- b_second: float32 [64], replicated, may hold values from -4 to 4
- w_out: float32 [64, 256], P(None, 'dp'), may hold values from -0.01171875 to 0.01171875
- rates: float32 [256], P('dp'), may hold values from 0.1 to 2
Outputs:
- gated_out: bfloat16 [16384, 4096], P('ctx', 'dp')
All inputs are finite; a program needn't handle non-finite values.
Results may differ from a plain program's by a relative error of at most 0.0061.
Values may be sent and summed in bfloat16 or wider, within the bound.
A program may use at most 64 MiB of HBM per device.

v0:
```python
import functools
import math

import jax
import jax.numpy as jnp
from jax import lax
from jax.experimental import pallas as pl
from jax.experimental.pallas import tpu as pltpu
from jax.sharding import PartitionSpec as P

MESH = pl.DeviceIdType.MESH
F32 = jnp.float32
BF16 = jnp.bfloat16
HIGHEST = lax.Precision.HIGHEST

TB = 256
CHAIN = 16

PI_A = 3.140625
PI_B = 9.67025756835938e-04
PI_C = 6.277114152908325e-07


def sine(x):
    turns = jnp.floor(x * (1.0 / math.pi) + 0.5)
    r = ((x - turns * PI_A) - turns * PI_B) - turns * PI_C
    odd = turns - 2.0 * jnp.floor(turns * 0.5)
    r = r * (1.0 - 2.0 * odd)
    r2 = r * r
    tail = -2.5052108e-8 + r2 * 1.6059044e-10
    tail = 2.7557319e-6 + r2 * tail
    tail = -1.9841270e-4 + r2 * tail
    tail = 8.3333333e-3 + r2 * tail
    tail = -1.6666667e-1 + r2 * tail
    return r + r * r2 * tail


def column(row):
    n = row.shape[1]
    square = jnp.broadcast_to(row, (n, n))
    at_row = lax.broadcasted_iota(jnp.int32, (n, n), 0)
    at_col = lax.broadcasted_iota(jnp.int32, (n, n), 1)
    return jnp.sum(jnp.where(at_row == at_col, square, 0.0), axis=1, keepdims=True)


def rows_to_rows(a, b):
    return lax.dot_general(
        a, b, (((0,), (0,)), ((), ())), precision=HIGHEST, preferred_element_type=F32
    )


def kernel(
    n,
    span,
    groups,
    size,
    q_hbm,
    k_hbm,
    v_hbm,
    taps_ref,
    skip_ref,
    freqs_ref,
    phases_ref,
    w1_ref,
    b1_ref,
    w2_ref,
    b2_ref,
    wo_ref,
    rates_ref,
    o_hbm,
    q_ref,
    k_ref,
    v_ref,
    o_ref,
    halo_ref,
    ext_ref,
    sig_ref,
    xs_ref,
    xa_ref,
    hs_ref,
    ha_ref,
    f_ref,
    acc_ref,
    ys_ref,
    yr_ref,
    in_sem,
    out_sem,
    halo_send,
    halo_recv,
    x_send,
    x_recv,
    h_send,
    h_recv,
    y_send,
    y_recv,
):
    me = lax.axis_index("ctx")
    seq = span * n
    blocks = span // TB
    piece = blocks * size
    pad = CHAIN * size

    def peer(j):
        return lax.rem(me + j, n)

    def source(j):
        return lax.rem(me + (n - j), n)

    load_v = pltpu.make_async_copy(v_hbm, v_ref, in_sem.at[0])
    load_k = pltpu.make_async_copy(k_hbm, k_ref, in_sem.at[1])
    load_q = pltpu.make_async_copy(q_hbm, q_ref, in_sem.at[2])
    load_v.start()
    load_k.start()
    load_q.start()

    barrier = pltpu.get_barrier_semaphore()
    for j in range(1, n):
        pl.semaphore_signal(
            barrier, inc=1, device_id={"ctx": peer(j)}, device_id_type=MESH
        )
    pl.semaphore_wait(barrier, n - 1)

    load_v.wait()
    halo = pltpu.make_async_remote_copy(
        src_ref=v_ref.at[pl.ds(span - 16, 16), :],
        dst_ref=halo_ref,
        send_sem=halo_send,
        recv_sem=halo_recv,
        device_id={"ctx": peer(1)},
        device_id_type=MESH,
    )
    halo.start()
    ext_ref[8:, :] = v_ref[...].astype(F32)
    load_k.wait()
    halo.wait()
    ext_ref[0:8, :] = jnp.where(me > 0, halo_ref[8:16, :].astype(F32), 0.0)

    taps = taps_ref[...]

    def one_block(a, _):
        at = pl.multiple_of(a * TB, TB)
        mixed = taps[0:1] * ext_ref[pl.ds(at + 8, TB), :]
        mixed = mixed + taps[1:2] * ext_ref[pl.ds(at + 7, TB), :]
        mixed = mixed + taps[2:3] * ext_ref[pl.ds(at + 6, TB), :]
        signal = (k_ref[pl.ds(at, TB), :].astype(F32) * mixed).astype(BF16)
        sig_ref[pl.ds(at, TB), :] = signal
        turned = signal.astype(F32).T.astype(BF16)
        row = pl.multiple_of(a * size, size)
        for g in range(groups):
            xs_ref[g, pl.ds(row, size), :] = turned[g * size : (g + 1) * size]
        return 0

    lax.fori_loop(0, blocks, one_block, 0)

    def x_copy(j):
        return pltpu.make_async_remote_copy(
            src_ref=xs_ref.at[peer(j)],
            dst_ref=xa_ref.at[pl.ds(pl.multiple_of(pad + me * piece, 16), piece), :],
            send_sem=x_send.at[j],
            recv_sem=x_recv.at[j],
            device_id={"ctx": peer(j)},
            device_id_type=MESH,
        )

    for j in range(1, n):
        x_copy(j).start()
    xa_ref[0:pad, :] = jnp.zeros((pad, TB), BF16)
    xa_ref[pl.ds(pl.multiple_of(pad + me * piece, 16), piece), :] = xs_ref[me]

    freq = column(freqs_ref[...]) * (2.0 * math.pi)
    phase = column(phases_ref[...])
    bias1 = column(b1_ref[...])
    bias2 = column(b2_ref[...])
    rate = column(rates_ref[...])
    wide = 512

    def some_positions(i, _):
        start = me * span + i * wide
        lanes = lax.broadcasted_iota(jnp.int32, (1, wide), 1) + start
        scaled = lanes.astype(F32) / seq
        feature = sine(freq * scaled + phase)
        first = sine(rows_to_rows(w1_ref[...], feature) + bias1)
        second = sine(rows_to_rows(w2_ref[...], first) + bias2)
        values = rows_to_rows(wo_ref[...], second) * jnp.exp(-rate * scaled)
        for t in range(wide // 128):
            for g in range(groups):
                hs_ref[g, pl.ds(i * (wide // 128) + t, 1), :] = values[
                    g : g + 1, t * 128 : (t + 1) * 128
                ]
        return 0

    lax.fori_loop(0, span // wide, some_positions, 0)

    tiles = span // 128

    def h_copy(j):
        return pltpu.make_async_remote_copy(
            src_ref=hs_ref.at[peer(j)],
            dst_ref=ha_ref.at[pl.ds(pl.multiple_of(me * tiles, 8), tiles), :],
            send_sem=h_send.at[j],
            recv_sem=h_recv.at[j],
            device_id={"ctx": peer(j)},
            device_id_type=MESH,
        )

    for j in range(1, n):
        h_copy(j).start()
    ha_ref[pl.ds(pl.multiple_of(me * tiles, 8), tiles), :] = hs_ref[me]
    for j in range(1, n):
        h_copy(j).wait()

    at_row = lax.broadcasted_iota(jnp.int32, (128, 128), 0)
    at_col = lax.broadcasted_iota(jnp.int32, (128, 128), 1)
    keep = at_col >= at_row
    f_ref[0] = jnp.zeros((128, 128), BF16)

    def one_tile(t, before):
        row = jnp.broadcast_to(ha_ref[pl.ds(t, 1), :], (128, 128))
        turned = pltpu.roll(row, 0, 1, stride=1, stride_axis=0)
        f_ref[t + 1] = jnp.where(keep, turned, before).astype(BF16)
        return turned

    lax.fori_loop(0, seq // 128, one_tile, jnp.zeros((128, 128), F32), unroll=2)

    for j in range(1, n):
        x_copy(j).wait()

    def lag_block(lag):
        low, mid, high = f_ref[2 * lag], f_ref[2 * lag + 1], f_ref[2 * lag + 2]
        return jnp.concatenate(
            [jnp.concatenate([mid, high], 1), jnp.concatenate([low, mid], 1)], 0
        )

    def y_copy(k, to, half, tile):
        j = lax.rem(to - me + n, n)
        return pltpu.make_async_remote_copy(
            src_ref=ys_ref.at[tile, pl.ds(half * piece, piece), :],
            dst_ref=yr_ref.at[me],
            send_sem=y_send.at[j],
            recv_sem=y_recv.at[j],
            device_id={"ctx": to},
            device_id_type=MESH,
        )

    tile_count = n // 2
    mine = me // 2
    half_me = lax.rem(me, 2)
    for k in range(tile_count):
        tile = lax.rem(mine + 1 + k, tile_count)
        acc_ref[...] = jnp.zeros_like(acc_ref)

        def lag_group(i, _, tile=tile):
            left, right = [], []
            for c in range(CHAIN):
                start = pad + (tile - i) * (2 * piece) - c * size
                left.append(xa_ref[pl.ds(pl.multiple_of(start, 16), 2 * piece), :])
                right.append(lag_block(i * CHAIN + c))
            acc_ref[...] += jnp.dot(
                jnp.concatenate(left, 1),
                jnp.concatenate(right, 0),
                preferred_element_type=F32,
            )
            return 0

        lax.fori_loop(0, tile + 1, lag_group, 0)
        ys_ref[tile] = acc_ref[...].astype(BF16)
        if k < tile_count - 1:
            y_copy(k, 2 * tile, 0, tile).start()
            y_copy(k, 2 * tile + 1, 1, tile).start()
        else:
            y_copy(k, 2 * tile + 1 - half_me, 1 - half_me, tile).start()
            yr_ref[me] = ys_ref[
                tile, pl.ds(pl.multiple_of(half_me * piece, 16), piece), :
            ]

    load_q.wait()
    for j in range(1, n):
        pltpu.make_async_remote_copy(
            src_ref=ys_ref.at[0, pl.ds(0, piece), :],
            dst_ref=yr_ref.at[source(j)],
            send_sem=y_send.at[j],
            recv_sem=y_recv.at[j],
            device_id={"ctx": peer(j)},
            device_id_type=MESH,
        ).wait()

    skip = skip_ref[...]

    def last_block(a, _):
        at = pl.multiple_of(a * TB, TB)
        row = pl.multiple_of(a * size, size)
        turned = jnp.concatenate(
            [yr_ref[g, pl.ds(row, size), :] for g in range(groups)], 0
        )
        conv = turned.astype(F32).T
        total = conv + skip * sig_ref[pl.ds(at, TB), :].astype(F32)
        o_ref[pl.ds(at, TB), :] = (
            q_ref[pl.ds(at, TB), :].astype(F32) * total
        ).astype(BF16)
        return 0

    lax.fori_loop(0, blocks, last_block, 0)
    store = pltpu.make_async_copy(o_ref, o_hbm, out_sem)
    store.start()
    store.wait()


def on_device(
    q_feat,
    k_feat,
    v_feat,
    short_taps,
    skip_bias,
    freqs,
    phases,
    w_first,
    b_first,
    w_second,
    b_second,
    w_out,
    rates,
):
    n = lax.axis_size("ctx")
    span, channels = q_feat.shape
    groups = rates.shape[0]
    size = channels // groups
    seq = span * n
    blocks = span // TB
    piece = blocks * size
    pad = CHAIN * size
    hbm = pl.BlockSpec(memory_space=pl.ANY)
    vmem = pl.BlockSpec(memory_space=pltpu.VMEM)
    dma = pltpu.SemaphoreType.DMA
    return pl.pallas_call(
        functools.partial(kernel, n, span, groups, size),
        name="toeplitz_conv",
        out_shape=jax.ShapeDtypeStruct((span, channels), BF16),
        in_specs=[hbm] * 3 + [vmem] * 10,
        out_specs=hbm,
        scratch_shapes=[
            pltpu.VMEM((span, channels), BF16),
            pltpu.VMEM((span, channels), BF16),
            pltpu.VMEM((span, channels), BF16),
            pltpu.VMEM((span, channels), BF16),
            pltpu.VMEM((16, channels), BF16),
            pltpu.VMEM((span + 8, channels), F32),
            pltpu.VMEM((span, channels), BF16),
            pltpu.VMEM((groups, piece, TB), BF16),
            pltpu.VMEM((pad + n * piece, TB), BF16),
            pltpu.VMEM((groups, span // 128, 128), F32),
            pltpu.VMEM((seq // 128, 128), F32),
            pltpu.VMEM((seq // 128 + 1, 128, 128), BF16),
            pltpu.VMEM((2 * piece, TB), F32),
            pltpu.VMEM((n // 2, 2 * piece, TB), BF16),
            pltpu.VMEM((groups, piece, TB), BF16),
            dma((3,)),
            dma,
            dma,
            dma,
            dma((n,)),
            dma((n,)),
            dma((n,)),
            dma((n,)),
            dma((n,)),
            dma((n,)),
        ],
        compiler_params=pltpu.CompilerParams(
            collective_id=0, has_side_effects=True, vmem_limit_bytes=40 << 20
        ),
    )(
        q_feat,
        k_feat,
        v_feat,
        short_taps,
        skip_bias.reshape(1, -1),
        freqs.reshape(1, -1),
        phases.reshape(1, -1),
        w_first,
        b_first.reshape(1, -1),
        w_second,
        b_second.reshape(1, -1),
        w_out,
        rates.reshape(1, -1),
    )


def solution(mesh):
    return jax.shard_map(
        on_device,
        mesh=mesh,
        in_specs=(
            P("ctx", "dp"),
            P("ctx", "dp"),
            P("ctx", "dp"),
            P(None, "dp"),
            P("dp"),
            P(),
            P(),
            P(),
            P(),
            P(),
            P(),
            P(None, "dp"),
            P("dp"),
        ),
        out_specs=P("ctx", "dp"),
        check_vma=False,
    )
```

profile of v0, /device:TPU:16, one launch (start us, length us, event | category | flops | bytes accessed | tf_op | source)
XLA Modules:
  0.0 40.8 jit_solution(3253526681815565095)
XLA Ops:
  0.0 0.0 copy-start.3
  0.0 0.0 copy-start.5
  0.0 0.0 copy-start.6
  0.0 0.0 copy-start.7
  0.0 0.0 copy-start.8
  0.0 0.0 copy-start.9
  0.0 0.0 copy-start.10
  0.0 0.0 copy-start.11
  0.1 0.8 %copy.14.wo_ref = f32[64,8]{1,0:T(8,128)S(1)} copy(f32[64,8]{0,1:T(8,128)} %param.24) | data formatting | bytes 4096 | tf_op args[11]
  0.9 0.0 copy-done.3
  0.9 0.0 copy-done.5
  0.9 0.0 copy-done.6
  0.9 0.0 copy-done.7
  0.9 0.0 copy-done.8
  0.9 0.0 copy-done.9
  0.9 0.0 copy-done.10
  1.0 0.0 copy-done.11
  1.0 0.0 copy-start
  1.0 1.0 %copy-done = bf16[2048,128]{1,0:T(8,128)(2,1)S(1)} copy-done((bf16[2048,128]{1,0:T(8,128)(2,1)S(1)}, bf16[2048,128]{1,0:T(8,128)(2,1)}, u32[]{:S(2)}) %copy-start) | copy-done | bytes 524312
  2.0 0.0 copy-start.1
  2.0 1.0 %copy-done.1 = bf16[2048,128]{1,0:T(8,128)(2,1)S(1)} copy-done((bf16[2048,128]{1,0:T(8,128)(2,1)S(1)}, bf16[2048,128]{1,0:T(8,128)(2,1)}, u32[]{:S(2)}) %copy-start.1) | copy-done | bytes 524312
  3.1 0.0 copy-start.2
  3.1 1.0 %copy-done.2 = bf16[2048,128]{1,0:T(8,128)(2,1)S(1)} copy-done((bf16[2048,128]{1,0:T(8,128)(2,1)S(1)}, bf16[2048,128]{1,0:T(8,128)(2,1)}, u32[]{:S(2)}) %copy-start.2) | copy-done | bytes 524312
  4.1 0.0 copy-start.4
  4.1 0.7 %copy-done.4 = f32[32,64]{1,0:T(8,128)S(1)} copy-done((f32[32,64]{1,0:T(8,128)S(1)}, f32[32,64]{1,0:T(8,128)}, u32[]{:S(2)}) %copy-start.4) | copy-done | bytes 8216
  4.8 35.2 %toeplitz_conv.1 = bf16[2048,128]{1,0:T(8,128)(2,1)S(1)} custom-call(bf16[2048,128]{1,0:T(8,128)(2,1)S(1)} %copy-done, bf16[2048,128]{1,0:T(8,128)(2,1)S(1)} %copy-done.1, bf16[2048,128]{1,0:T(8,128)(2,1)S(1)} %copy-done.2, f32[3,128]{1,0:T(4,128)S(1)} %copy-done.5, f32[1,128]{1,0:T(1,128)S(1)} %bitcast.6, f32[1,32]{1,0:T(1,128)S(1)} %bitcast.7, ...), custom_call_target="tpu_custom_call" | custom-call | tf_op jit(solution)/shard_map/toeplitz_conv/pallas_call | solution.py:334
  40.1 0.8 %copy.16 = bf16[2048,128]{1,0:T(8,128)(2,1)} copy(bf16[2048,128]{1,0:T(8,128)(2,1)S(1)} %toeplitz_conv.1) | data formatting | bytes 1048576
Async XLA Ops:
  0.0 0.9 %copy-start.3 = (f32[64,64]{1,0:T(8,128)S(1)}, f32[64,64]{1,0:T(8,128)}, u32[]{:S(2)}) copy-start(f32[64,64]{1,0:T(8,128)} %w2_ref.1) | copy-start | bytes 49156
  0.0 0.9 %copy-start.5 = (f32[3,128]{1,0:T(4,128)S(1)}, f32[3,128]{1,0:T(4,128)}, u32[]{:S(2)}) copy-start(f32[3,128]{1,0:T(4,128)} %taps_ref.1) | copy-start | bytes 4612
  0.0 0.9 %copy-start.6 = (f32[128]{0:T(128)S(1)}, f32[128]{0:T(128)}, u32[]{:S(2)}) copy-start(f32[128]{0:T(128)} %param.17) | copy-start | bytes 1540
  0.0 0.9 %copy-start.7 = (f32[32]{0:T(128)S(1)}, f32[32]{0:T(128)}, u32[]{:S(2)}) copy-start(f32[32]{0:T(128)} %param.18) | copy-start | bytes 388
  0.0 0.9 %copy-start.8 = (f32[32]{0:T(128)S(1)}, f32[32]{0:T(128)}, u32[]{:S(2)}) copy-start(f32[32]{0:T(128)} %param.19) | copy-start | bytes 388
  0.0 0.9 %copy-start.9 = (f32[64]{0:T(128)S(1)}, f32[64]{0:T(128)}, u32[]{:S(2)}) copy-start(f32[64]{0:T(128)} %param.21) | copy-start | bytes 772
  0.0 0.9 %copy-start.10 = (f32[64]{0:T(128)S(1)}, f32[64]{0:T(128)}, u32[]{:S(2)}) copy-start(f32[64]{0:T(128)} %param.23) | copy-start | bytes 772
  0.0 0.9 %copy-start.11 = (f32[8]{0:T(128)S(1)}, f32[8]{0:T(128)}, u32[]{:S(2)}) copy-start(f32[8]{0:T(128)} %param.25) | copy-start | bytes 100
  1.0 1.0 %copy-start = (bf16[2048,128]{1,0:T(8,128)(2,1)S(1)}, bf16[2048,128]{1,0:T(8,128)(2,1)}, u32[]{:S(2)}) copy-start(bf16[2048,128]{1,0:T(8,128)(2,1)} %q_hbm.1) | copy-start | bytes 1572868
  2.0 1.0 %copy-start.1 = (bf16[2048,128]{1,0:T(8,128)(2,1)S(1)}, bf16[2048,128]{1,0:T(8,128)(2,1)}, u32[]{:S(2)}) copy-start(bf16[2048,128]{1,0:T(8,128)(2,1)} %k_hbm.1) | copy-start | bytes 1572868
  3.1 1.0 %copy-start.2 = (bf16[2048,128]{1,0:T(8,128)(2,1)S(1)}, bf16[2048,128]{1,0:T(8,128)(2,1)}, u32[]{:S(2)}) copy-start(bf16[2048,128]{1,0:T(8,128)(2,1)} %v_hbm.1) | copy-start | bytes 1572868
  4.1 0.7 %copy-start.4 = (f32[32,64]{1,0:T(8,128)S(1)}, f32[32,64]{1,0:T(8,128)}, u32[]{:S(2)}) copy-start(f32[32,64]{1,0:T(8,128)} %w1_ref.1) | copy-start | bytes 24580
where the time goes:
time: 41.2 us; the launch traced here: 40.8 us
  Pallas kernels  35.2 us (85%)
  local copies, waits for them, and re-layouts  5.5 us (13%)
    pallas_call x1, Pallas kernels, on_device(): pl.pallas_call(functools.partial(kernel, n, span, groups, size), name='to...  35.2 us
    unnamed x26, local copies, waits for them, and re-layouts  5.5 us

commit v1 on v0

--- a/solution.py
+++ b/solution.py
@@ -57,6 +57,17 @@
     q_hbm,
     k_hbm,
     v_hbm,
+    taps_hbm,
+    skip_hbm,
+    freqs_hbm,
+    phases_hbm,
+    w1_hbm,
+    b1_hbm,
+    w2_hbm,
+    b2_hbm,
+    wo_hbm,
+    rates_hbm,
+    o_ref,
     taps_ref,
     skip_ref,
     freqs_ref,
@@ -67,11 +78,9 @@
     b2_ref,
     wo_ref,
     rates_ref,
-    o_hbm,
     q_ref,
     k_ref,
     v_ref,
-    o_ref,
     halo_ref,
     ext_ref,
     sig_ref,
@@ -80,11 +89,10 @@
     hs_ref,
     ha_ref,
     f_ref,
-    acc_ref,
     ys_ref,
     yr_ref,
     in_sem,
-    out_sem,
+    small_sem,
     halo_send,
     halo_recv,
     x_send,
@@ -111,30 +119,37 @@
     load_q = pltpu.make_async_copy(q_hbm, q_ref, in_sem.at[2])
     load_v.start()
     load_k.start()
-    load_q.start()
-
+    loads = [
+        pltpu.make_async_copy(src, dst, small_sem.at[i])
+        for i, (src, dst) in enumerate(
+            [
+                (taps_hbm, taps_ref),
+                (skip_hbm, skip_ref),
+                (freqs_hbm, freqs_ref),
+                (phases_hbm, phases_ref),
+                (w1_hbm, w1_ref),
+                (b1_hbm, b1_ref),
+                (w2_hbm, w2_ref),
+                (b2_hbm, b2_ref),
+                (wo_hbm, wo_ref),
+                (rates_hbm, rates_ref),
+            ]
+        )
+    ]
     barrier = pltpu.get_barrier_semaphore()
     for j in range(1, n):
         pl.semaphore_signal(
             barrier, inc=1, device_id={"ctx": peer(j)}, device_id_type=MESH
         )
-    pl.semaphore_wait(barrier, n - 1)
+    for load in loads:
+        load.start()
+    load_q.start()
 
     load_v.wait()
-    halo = pltpu.make_async_remote_copy(
-        src_ref=v_ref.at[pl.ds(span - 16, 16), :],
-        dst_ref=halo_ref,
-        send_sem=halo_send,
-        recv_sem=halo_recv,
-        device_id={"ctx": peer(1)},
-        device_id_type=MESH,
-    )
-    halo.start()
     ext_ref[8:, :] = v_ref[...].astype(F32)
+    ext_ref[0:8, :] = jnp.zeros((8, groups * size), F32)
+    loads[0].wait()
     load_k.wait()
-    halo.wait()
-    ext_ref[0:8, :] = jnp.where(me > 0, halo_ref[8:16, :].astype(F32), 0.0)
-
     taps = taps_ref[...]
 
     def one_block(a, _):
@@ -150,23 +165,44 @@
             xs_ref[g, pl.ds(row, size), :] = turned[g * size : (g + 1) * size]
         return 0
 
-    lax.fori_loop(0, blocks, one_block, 0)
-
-    def x_copy(j):
+    lax.fori_loop(1, blocks, one_block, 0)
+    pl.semaphore_wait(barrier, n - 1)
+
+    halo = pltpu.make_async_remote_copy(
+        src_ref=v_ref.at[pl.ds(span - 16, 16), :],
+        dst_ref=halo_ref,
+        send_sem=halo_send,
+        recv_sem=halo_recv,
+        device_id={"ctx": peer(1)},
+        device_id_type=MESH,
+    )
+    halo.start()
+
+    half = piece // 2
+
+    def x_copy(j, part):
+        at = pad + me * piece + part * half
         return pltpu.make_async_remote_copy(
-            src_ref=xs_ref.at[peer(j)],
-            dst_ref=xa_ref.at[pl.ds(pl.multiple_of(pad + me * piece, 16), piece), :],
-            send_sem=x_send.at[j],
-            recv_sem=x_recv.at[j],
+            src_ref=xs_ref.at[peer(j), pl.ds(part * half, half), :],
+            dst_ref=xa_ref.at[pl.ds(pl.multiple_of(at, 16), half), :],
+            send_sem=x_send.at[part, j],
+            recv_sem=x_recv.at[part, j],
             device_id={"ctx": peer(j)},
             device_id_type=MESH,
         )
 
     for j in range(1, n):
-        x_copy(j).start()
+        x_copy(j, 1).start()
     xa_ref[0:pad, :] = jnp.zeros((pad, TB), BF16)
+    halo.wait()
+    ext_ref[0:8, :] = jnp.where(me > 0, halo_ref[8:16, :].astype(F32), 0.0)
+    one_block(0, 0)
+    for j in range(1, n):
+        x_copy(j, 0).start()
     xa_ref[pl.ds(pl.multiple_of(pad + me * piece, 16), piece), :] = xs_ref[me]
 
+    for load in loads[1:]:
+        load.wait()
     freq = column(freqs_ref[...]) * (2.0 * math.pi)
     phase = column(phases_ref[...])
     bias1 = column(b1_ref[...])
@@ -181,7 +217,9 @@
         feature = sine(freq * scaled + phase)
         first = sine(rows_to_rows(w1_ref[...], feature) + bias1)
         second = sine(rows_to_rows(w2_ref[...], first) + bias2)
-        values = rows_to_rows(wo_ref[...], second) * jnp.exp(-rate * scaled)
+        values = lax.dot(
+            wo_ref[...], second, precision=HIGHEST, preferred_element_type=F32
+        ) * jnp.exp(-rate * scaled)
         for t in range(wide // 128):
             for g in range(groups):
                 hs_ref[g, pl.ds(i * (wide // 128) + t, 1), :] = values[
@@ -220,10 +258,20 @@
         f_ref[t + 1] = jnp.where(keep, turned, before).astype(BF16)
         return turned
 
-    lax.fori_loop(0, seq // 128, one_tile, jnp.zeros((128, 128), F32), unroll=2)
-
-    for j in range(1, n):
-        x_copy(j).wait()
+    lax.fori_loop(0, seq // 128, one_tile, jnp.zeros((128, 128), F32), unroll=32)
+
+    def x_wait(s):
+        j = lax.rem(me - s + n, n)
+        for part in (1, 0):
+            at = pad + s * piece + part * half
+            pltpu.make_async_remote_copy(
+                src_ref=xs_ref.at[s, pl.ds(part * half, half), :],
+                dst_ref=xa_ref.at[pl.ds(pl.multiple_of(at, 16), half), :],
+                send_sem=x_send.at[part, j],
+                recv_sem=x_recv.at[part, j],
+                device_id={"ctx": s},
+                device_id_type=MESH,
+            ).wait_recv()
 
     def lag_block(lag):
         low, mid, high = f_ref[2 * lag], f_ref[2 * lag + 1], f_ref[2 * lag + 2]
@@ -231,10 +279,10 @@
             [jnp.concatenate([mid, high], 1), jnp.concatenate([low, mid], 1)], 0
         )
 
-    def y_copy(k, to, half, tile):
+    def y_copy(to):
         j = lax.rem(to - me + n, n)
         return pltpu.make_async_remote_copy(
-            src_ref=ys_ref.at[tile, pl.ds(half * piece, piece), :],
+            src_ref=ys_ref.at[to],
             dst_ref=yr_ref.at[me],
             send_sem=y_send.at[j],
             recv_sem=y_recv.at[j],
@@ -242,41 +290,52 @@
             device_id_type=MESH,
         )
 
-    tile_count = n // 2
-    mine = me // 2
-    half_me = lax.rem(me, 2)
-    for k in range(tile_count):
-        tile = lax.rem(mine + 1 + k, tile_count)
-        acc_ref[...] = jnp.zeros_like(acc_ref)
-
-        def lag_group(i, _, tile=tile):
-            left, right = [], []
-            for c in range(CHAIN):
-                start = pad + (tile - i) * (2 * piece) - c * size
-                left.append(xa_ref[pl.ds(pl.multiple_of(start, 16), 2 * piece), :])
-                right.append(lag_block(i * CHAIN + c))
-            acc_ref[...] += jnp.dot(
-                jnp.concatenate(left, 1),
-                jnp.concatenate(right, 0),
-                preferred_element_type=F32,
-            )
-            return 0
-
-        lax.fori_loop(0, tile + 1, lag_group, 0)
-        ys_ref[tile] = acc_ref[...].astype(BF16)
-        if k < tile_count - 1:
-            y_copy(k, 2 * tile, 0, tile).start()
-            y_copy(k, 2 * tile + 1, 1, tile).start()
-        else:
-            y_copy(k, 2 * tile + 1 - half_me, 1 - half_me, tile).start()
-            yr_ref[me] = ys_ref[
-                tile, pl.ds(pl.multiple_of(half_me * piece, 16), piece), :
-            ]
+    def one_source(s, _):
+        x_wait(s)
+        return 0
+
+    lax.fori_loop(0, me, one_source, 0)
+
+    def one_span(k, _):
+        to = lax.rem(me + 1 + k, n)
+
+        @pl.when(to > me)
+        def _():
+            x_wait(to)
+
+        for c in range(n):
+
+            @pl.when(to == c)
+            def _(c=c):
+                left, right = [], []
+                for lag in range((c + 1) * blocks):
+                    start = pad + c * piece - lag * size
+                    if start + piece <= pad:
+                        break
+                    left.append(xa_ref[start : start + piece, :])
+                    right.append(lag_block(lag))
+                ys_ref[c] = jnp.dot(
+                    jnp.concatenate(left, 1),
+                    jnp.concatenate(right, 0),
+                    preferred_element_type=F32,
+                ).astype(BF16)
+
+        @pl.when(to != me)
+        def _():
+            y_copy(to).start()
+
+        return 0
+
+    lax.fori_loop(0, n, one_span, 0)
+    yr_ref[me] = ys_ref[me]
+    for j in range(1, n):
+        for part in (1, 0):
+            x_copy(j, part).wait_send()
 
     load_q.wait()
     for j in range(1, n):
         pltpu.make_async_remote_copy(
-            src_ref=ys_ref.at[0, pl.ds(0, piece), :],
+            src_ref=ys_ref.at[peer(j)],
             dst_ref=yr_ref.at[source(j)],
             send_sem=y_send.at[j],
             recv_sem=y_recv.at[j],
@@ -300,9 +359,6 @@
         return 0
 
     lax.fori_loop(0, blocks, last_block, 0)
-    store = pltpu.make_async_copy(o_ref, o_hbm, out_sem)
-    store.start()
-    store.wait()
 
 
 def on_device(
@@ -335,10 +391,19 @@
         functools.partial(kernel, n, span, groups, size),
         name="toeplitz_conv",
         out_shape=jax.ShapeDtypeStruct((span, channels), BF16),
-        in_specs=[hbm] * 3 + [vmem] * 10,
-        out_specs=hbm,
+        in_specs=[hbm] * 13,
+        out_specs=vmem,
         scratch_shapes=[
-            pltpu.VMEM((span, channels), BF16),
+            pltpu.VMEM(short_taps.shape, F32),
+            pltpu.VMEM((1, channels), F32),
+            pltpu.VMEM((1, freqs.shape[0]), F32),
+            pltpu.VMEM((1, phases.shape[0]), F32),
+            pltpu.VMEM(w_first.shape, F32),
+            pltpu.VMEM((1, b_first.shape[0]), F32),
+            pltpu.VMEM(w_second.shape, F32),
+            pltpu.VMEM((1, b_second.shape[0]), F32),
+            pltpu.VMEM((groups, w_out.shape[0]), F32),
+            pltpu.VMEM((1, groups), F32),
             pltpu.VMEM((span, channels), BF16),
             pltpu.VMEM((span, channels), BF16),
             pltpu.VMEM((span, channels), BF16),
@@ -350,22 +415,21 @@
             pltpu.VMEM((groups, span // 128, 128), F32),
             pltpu.VMEM((seq // 128, 128), F32),
             pltpu.VMEM((seq // 128 + 1, 128, 128), BF16),
-            pltpu.VMEM((2 * piece, TB), F32),
-            pltpu.VMEM((n // 2, 2 * piece, TB), BF16),
+            pltpu.VMEM((n, piece, TB), BF16),
             pltpu.VMEM((groups, piece, TB), BF16),
             dma((3,)),
+            dma((10,)),
             dma,
             dma,
-            dma,
-            dma((n,)),
-            dma((n,)),
+            dma((2, n)),
+            dma((2, n)),
             dma((n,)),
             dma((n,)),
             dma((n,)),
             dma((n,)),
         ],
         compiler_params=pltpu.CompilerParams(
-            collective_id=0, has_side_effects=True, vmem_limit_bytes=40 << 20
+            collective_id=0, has_side_effects=True, vmem_limit_bytes=62 << 20
         ),
     )(
         q_feat,
@@ -379,7 +443,7 @@
         b_first.reshape(1, -1),
         w_second,
         b_second.reshape(1, -1),
-        w_out,
+        w_out.T,
         rates.reshape(1, -1),
     )
 

time: 41.2 us -> 31.2 us (0.76)
  Pallas kernels: 35.2 us -> 29.2 us
  local copies, waits for them, and re-layouts: 5.5 us -> 1.87 us
    pallas_call x1, Pallas kernels: 35.2 us -> 29.2 us  [on_device(): pl.pallas_call(functools.partial(kernel, n, span, groups, size), name='to...]
    unnamed x26 -> x1, local copies, waits for them, and re-layouts: 5.5 us -> 1.87 us
where the time goes in v1:
time: 31.2 us; the launch traced here: 31.1 us
  Pallas kernels  29.2 us (94%)
  local copies, waits for them, and re-layouts  1.87 us (6%)
    pallas_call x1, Pallas kernels, on_device(): pl.pallas_call(functools.partial(kernel, n, span, groups, size), name='to...  29.2 us
    unnamed x1, local copies, waits for them, and re-layouts  1.87 us

profile of v1, /device:TPU:16, one launch (start us, length us, event | category | flops | bytes accessed | tf_op | source)
XLA Modules:
  0.0 31.1 jit_solution(719978076402232964)
XLA Ops:
  0.0 29.2 %toeplitz_conv.1 = bf16[2048,128]{1,0:T(8,128)(2,1)} custom-call(bf16[2048,128]{1,0:T(8,128)(2,1)} %q_hbm.1, bf16[2048,128]{1,0:T(8,128)(2,1)} %k_hbm.1, bf16[2048,128]{1,0:T(8,128)(2,1)} %v_hbm.1, f32[3,128]{1,0:T(4,128)} %taps_hbm.1, f32[1,128]{1,0:T(1,128)} %bitcast.8, f32[1,32]{1,0:T(1,128)} %bitcast.9, f32[1,32]{1,0:T(1,128)} %bitcast.10, ...), custom_call_target="tpu_custom_call" | custom-call | tf_op jit(solution)/shard_map/toeplitz_conv/pallas_call | solution.py:390
  29.2 1.9 %copy.15 = bf16[2048,128]{1,0:T(8,128)(2,1)} copy(bf16[2048,128]{1,0:T(8,128)(2,1)} %toeplitz_conv.1) | data formatting | bytes 1048576

commit v2 on v1

--- a/solution.py
+++ b/solution.py
@@ -85,7 +85,8 @@
     ext_ref,
     sig_ref,
     xs_ref,
-    xa_ref,
+    xe_ref,
+    xo_ref,
     hs_ref,
     ha_ref,
     f_ref,
@@ -105,8 +106,9 @@
     me = lax.axis_index("ctx")
     seq = span * n
     blocks = span // TB
-    piece = blocks * size
-    pad = CHAIN * size
+    rows = size // 2
+    part = blocks * rows
+    pad = CHAIN * rows
 
     def peer(j):
         return lax.rem(me + j, n)
@@ -117,6 +119,11 @@
     load_v = pltpu.make_async_copy(v_hbm, v_ref, in_sem.at[0])
     load_k = pltpu.make_async_copy(k_hbm, k_ref, in_sem.at[1])
     load_q = pltpu.make_async_copy(q_hbm, q_ref, in_sem.at[2])
+    barrier = pltpu.get_barrier_semaphore()
+    for j in range(1, n):
+        pl.semaphore_signal(
+            barrier, inc=1, device_id={"ctx": peer(j)}, device_id_type=MESH
+        )
     load_v.start()
     load_k.start()
     loads = [
@@ -136,38 +143,14 @@
             ]
         )
     ]
-    barrier = pltpu.get_barrier_semaphore()
-    for j in range(1, n):
-        pl.semaphore_signal(
-            barrier, inc=1, device_id={"ctx": peer(j)}, device_id_type=MESH
-        )
     for load in loads:
         load.start()
     load_q.start()
+    for h in range(2):
+        xe_ref[h, 0:pad, :] = jnp.zeros((pad, TB), BF16)
 
     load_v.wait()
-    ext_ref[8:, :] = v_ref[...].astype(F32)
-    ext_ref[0:8, :] = jnp.zeros((8, groups * size), F32)
-    loads[0].wait()
-    load_k.wait()
-    taps = taps_ref[...]
-
-    def one_block(a, _):
-        at = pl.multiple_of(a * TB, TB)
-        mixed = taps[0:1] * ext_ref[pl.ds(at + 8, TB), :]
-        mixed = mixed + taps[1:2] * ext_ref[pl.ds(at + 7, TB), :]
-        mixed = mixed + taps[2:3] * ext_ref[pl.ds(at + 6, TB), :]
-        signal = (k_ref[pl.ds(at, TB), :].astype(F32) * mixed).astype(BF16)
-        sig_ref[pl.ds(at, TB), :] = signal
-        turned = signal.astype(F32).T.astype(BF16)
-        row = pl.multiple_of(a * size, size)
-        for g in range(groups):
-            xs_ref[g, pl.ds(row, size), :] = turned[g * size : (g + 1) * size]
-        return 0
-
-    lax.fori_loop(1, blocks, one_block, 0)
     pl.semaphore_wait(barrier, n - 1)
-
     halo = pltpu.make_async_remote_copy(
         src_ref=v_ref.at[pl.ds(span - 16, 16), :],
         dst_ref=halo_ref,
@@ -178,28 +161,60 @@
     )
     halo.start()
 
-    half = piece // 2
-
-    def x_copy(j, part):
-        at = pad + me * piece + part * half
+    ext_ref[8:, :] = v_ref[...].astype(F32)
+    loads[0].wait()
+    load_k.wait()
+    taps = taps_ref[...]
+
+    def one_pair(i, _):
+        turned = []
+        for u in range(2):
+            at = pl.multiple_of((2 * i + u) * TB, TB)
+            mixed = taps[0:1] * ext_ref[pl.ds(at + 8, TB), :]
+            mixed = mixed + taps[1:2] * ext_ref[pl.ds(at + 7, TB), :]
+            mixed = mixed + taps[2:3] * ext_ref[pl.ds(at + 6, TB), :]
+            signal = (k_ref[pl.ds(at, TB), :].astype(F32) * mixed).astype(BF16)
+            sig_ref[pl.ds(at, TB), :] = signal
+            turned.append(signal.astype(F32).T)
+        for g in range(groups):
+            for h in range(2):
+                low = g * size + h * rows
+                row = pl.multiple_of(h * part + i * size, size)
+                xs_ref[g, pl.ds(row, size), :] = jnp.concatenate(
+                    [turned[0][low : low + rows], turned[1][low : low + rows]], 0
+                ).astype(BF16)
+        return 0
+
+    lax.fori_loop(1, blocks // 2, one_pair, 0)
+
+    parts = [(0, size, part - size), (0, 0, size), (1, 0, part)]
+
+    def x_copy(j, p):
+        h, first, count = parts[p]
+        at = pl.multiple_of(pad + me * part + first, 16)
         return pltpu.make_async_remote_copy(
-            src_ref=xs_ref.at[peer(j), pl.ds(part * half, half), :],
-            dst_ref=xa_ref.at[pl.ds(pl.multiple_of(at, 16), half), :],
-            send_sem=x_send.at[part, j],
-            recv_sem=x_recv.at[part, j],
+            src_ref=xs_ref.at[peer(j), pl.ds(h * part + first, count), :],
+            dst_ref=xe_ref.at[h, pl.ds(at, count), :],
+            send_sem=x_send.at[p, j],
+            recv_sem=x_recv.at[p, j],
             device_id={"ctx": peer(j)},
             device_id_type=MESH,
         )
 
-    for j in range(1, n):
-        x_copy(j, 1).start()
-    xa_ref[0:pad, :] = jnp.zeros((pad, TB), BF16)
-    halo.wait()
-    ext_ref[0:8, :] = jnp.where(me > 0, halo_ref[8:16, :].astype(F32), 0.0)
-    one_block(0, 0)
+    def x_wait(j, p):
+        h, first, count = parts[p]
+        at = pl.multiple_of(pad + source(j) * part + first, 16)
+        pltpu.make_async_remote_copy(
+            src_ref=xs_ref.at[peer(j), pl.ds(h * part + first, count), :],
+            dst_ref=xe_ref.at[h, pl.ds(at, count), :],
+            send_sem=x_send.at[p, j],
+            recv_sem=x_recv.at[p, j],
+            device_id={"ctx": peer(j)},
+            device_id_type=MESH,
+        ).wait()
+
     for j in range(1, n):
         x_copy(j, 0).start()
-    xa_ref[pl.ds(pl.multiple_of(pad + me * piece, 16), piece), :] = xs_ref[me]
 
     for load in loads[1:]:
         load.wait()
@@ -208,7 +223,7 @@
     bias1 = column(b1_ref[...])
     bias2 = column(b2_ref[...])
     rate = column(rates_ref[...])
-    wide = 512
+    wide = span
 
     def some_positions(i, _):
         start = me * span + i * wide
@@ -241,8 +256,18 @@
             device_id_type=MESH,
         )
 
+    halo.wait()
+    ext_ref[0:8, :] = jnp.where(me > 0, halo_ref[8:16, :].astype(F32), 0.0)
+    one_pair(0, 0)
+    for j in range(1, n):
+        x_copy(j, 1).start()
     for j in range(1, n):
         h_copy(j).start()
+    for j in range(1, n):
+        x_copy(j, 2).start()
+    for h in range(2):
+        at = pl.multiple_of(pad + me * part, 16)
+        xe_ref[h, pl.ds(at, part), :] = xs_ref[me, h * part : (h + 1) * part, :]
     ha_ref[pl.ds(pl.multiple_of(me * tiles, 8), tiles), :] = hs_ref[me]
     for j in range(1, n):
         h_copy(j).wait()
@@ -260,105 +285,100 @@
 
     lax.fori_loop(0, seq // 128, one_tile, jnp.zeros((128, 128), F32), unroll=32)
 
-    def x_wait(s):
-        j = lax.rem(me - s + n, n)
-        for part in (1, 0):
-            at = pad + s * piece + part * half
-            pltpu.make_async_remote_copy(
-                src_ref=xs_ref.at[s, pl.ds(part * half, half), :],
-                dst_ref=xa_ref.at[pl.ds(pl.multiple_of(at, 16), half), :],
-                send_sem=x_send.at[part, j],
-                recv_sem=x_recv.at[part, j],
-                device_id={"ctx": s},
-                device_id_type=MESH,
-            ).wait_recv()
-
     def lag_block(lag):
         low, mid, high = f_ref[2 * lag], f_ref[2 * lag + 1], f_ref[2 * lag + 2]
         return jnp.concatenate(
             [jnp.concatenate([mid, high], 1), jnp.concatenate([low, mid], 1)], 0
         )
 
-    def y_copy(to):
+    def y_copy(h, to):
         j = lax.rem(to - me + n, n)
         return pltpu.make_async_remote_copy(
-            src_ref=ys_ref.at[to],
-            dst_ref=yr_ref.at[me],
-            send_sem=y_send.at[j],
-            recv_sem=y_recv.at[j],
+            src_ref=ys_ref.at[h, to],
+            dst_ref=yr_ref.at[h, me],
+            send_sem=y_send.at[h, j],
+            recv_sem=y_recv.at[h, j],
             device_id={"ctx": to},
             device_id_type=MESH,
         )
 
-    def one_source(s, _):
-        x_wait(s)
+    pairs = n // 2
+    wide_rows = 2 * part
+    for h in range(2):
+        for p in range(3):
+            if parts[p][0] == h:
+                for j in range(1, n):
+                    x_wait(j, p)
+        whole = xe_ref[h].astype(F32)
+        xo_ref[h] = jnp.concatenate(
+            [jnp.zeros((rows, TB), F32), whole[: whole.shape[0] - rows]], 0
+        ).astype(BF16)
+
+        def one_pair_of_spans(k, _, h=h):
+            two = lax.rem(me // 2 + 1 + k, pairs)
+            for c in range(pairs):
+
+                @pl.when(two == c)
+                def _(c=c):
+                    left, right = [], []
+                    for lag in range((c + 1) * CHAIN):
+                        start = pad + c * wide_rows - lag * rows
+                        if start % 16 == 0:
+                            left.append(xe_ref[h, start : start + wide_rows, :])
+                        else:
+                            start = start + rows
+                            left.append(xo_ref[h, start : start + wide_rows, :])
+                        right.append(lag_block(lag))
+                    out = jnp.dot(
+                        jnp.concatenate(left, 1),
+                        jnp.concatenate(right, 0),
+                        preferred_element_type=F32,
+                    ).astype(BF16)
+                    ys_ref[h, 2 * c] = out[:part]
+                    ys_ref[h, 2 * c + 1] = out[part:]
+
+            @pl.when(k < pairs - 1)
+            def _():
+                y_copy(h, 2 * two).start()
+                y_copy(h, 2 * two + 1).start()
+
+            return 0
+
+        lax.fori_loop(0, pairs, one_pair_of_spans, 0)
+        y_copy(h, me + 1 - 2 * lax.rem(me, 2)).start()
+        yr_ref[h, me] = ys_ref[h, me]
+
+    load_q.wait()
+    for h in range(2):
+        for j in range(1, n):
+            pltpu.make_async_remote_copy(
+                src_ref=ys_ref.at[h, peer(j)],
+                dst_ref=yr_ref.at[h, source(j)],
+                send_sem=y_send.at[h, j],
+                recv_sem=y_recv.at[h, j],
+                device_id={"ctx": peer(j)},
+                device_id_type=MESH,
+            ).wait()
+
+    skip = skip_ref[...]
+
+    def last_pair(i, _):
+        row = pl.multiple_of(i * size, size)
+        two = [
+            yr_ref[h, g, pl.ds(row, size), :].astype(F32)
+            for g in range(groups)
+            for h in range(2)
+        ]
+        for u in range(2):
+            at = pl.multiple_of((2 * i + u) * TB, TB)
+            conv = jnp.concatenate([x[u * rows : (u + 1) * rows] for x in two], 0).T
+            total = conv + skip * sig_ref[pl.ds(at, TB), :].astype(F32)
+            o_ref[pl.ds(at, TB), :] = (
+                q_ref[pl.ds(at, TB), :].astype(F32) * total
+            ).astype(BF16)
         return 0
 
-    lax.fori_loop(0, me, one_source, 0)
-
-    def one_span(k, _):
-        to = lax.rem(me + 1 + k, n)
-
-        @pl.when(to > me)
-        def _():
-            x_wait(to)
-
-        for c in range(n):
-
-            @pl.when(to == c)
-            def _(c=c):
-                left, right = [], []
-                for lag in range((c + 1) * blocks):
-                    start = pad + c * piece - lag * size
-                    if start + piece <= pad:
-                        break
-                    left.append(xa_ref[start : start + piece, :])
-                    right.append(lag_block(lag))
-                ys_ref[c] = jnp.dot(
-                    jnp.concatenate(left, 1),
-                    jnp.concatenate(right, 0),
-                    preferred_element_type=F32,
-                ).astype(BF16)
-
-        @pl.when(to != me)
-        def _():
-            y_copy(to).start()
-
-        return 0
-
-    lax.fori_loop(0, n, one_span, 0)
-    yr_ref[me] = ys_ref[me]
-    for j in range(1, n):
-        for part in (1, 0):
-            x_copy(j, part).wait_send()
-
-    load_q.wait()
-    for j in range(1, n):
-        pltpu.make_async_remote_copy(
-            src_ref=ys_ref.at[peer(j)],
-            dst_ref=yr_ref.at[source(j)],
-            send_sem=y_send.at[j],
-            recv_sem=y_recv.at[j],
-            device_id={"ctx": peer(j)},
-            device_id_type=MESH,
-        ).wait()
-
-    skip = skip_ref[...]
-
-    def last_block(a, _):
-        at = pl.multiple_of(a * TB, TB)
-        row = pl.multiple_of(a * size, size)
-        turned = jnp.concatenate(
-            [yr_ref[g, pl.ds(row, size), :] for g in range(groups)], 0
-        )
-        conv = turned.astype(F32).T
-        total = conv + skip * sig_ref[pl.ds(at, TB), :].astype(F32)
-        o_ref[pl.ds(at, TB), :] = (
-            q_ref[pl.ds(at, TB), :].astype(F32) * total
-        ).astype(BF16)
-        return 0
-
-    lax.fori_loop(0, blocks, last_block, 0)
+    lax.fori_loop(0, blocks // 2, last_pair, 0)
 
 
 def on_device(
@@ -383,14 +403,15 @@
     seq = span * n
     blocks = span // TB
     piece = blocks * size
-    pad = CHAIN * size
-    hbm = pl.BlockSpec(memory_space=pl.ANY)
+    part = piece // 2
+    pad = CHAIN * size // 2
+    hbm = pl.BlockSpec(memory_space=pltpu.HBM)
     vmem = pl.BlockSpec(memory_space=pltpu.VMEM)
     dma = pltpu.SemaphoreType.DMA
     return pl.pallas_call(
         functools.partial(kernel, n, span, groups, size),
         name="toeplitz_conv",
-        out_shape=jax.ShapeDtypeStruct((span, channels), BF16),
+        out_shape=pltpu.VMEM((span, channels), BF16),
         in_specs=[hbm] * 13,
         out_specs=vmem,
         scratch_shapes=[
@@ -411,22 +432,23 @@
             pltpu.VMEM((span + 8, channels), F32),
             pltpu.VMEM((span, channels), BF16),
             pltpu.VMEM((groups, piece, TB), BF16),
-            pltpu.VMEM((pad + n * piece, TB), BF16),
+            pltpu.VMEM((2, pad + n * part, TB), BF16),
+            pltpu.VMEM((2, pad + n * part, TB), BF16),
             pltpu.VMEM((groups, span // 128, 128), F32),
             pltpu.VMEM((seq // 128, 128), F32),
             pltpu.VMEM((seq // 128 + 1, 128, 128), BF16),
-            pltpu.VMEM((n, piece, TB), BF16),
-            pltpu.VMEM((groups, piece, TB), BF16),
+            pltpu.VMEM((2, n, part, TB), BF16),
+            pltpu.VMEM((2, groups, part, TB), BF16),
             dma((3,)),
             dma((10,)),
             dma,
             dma,
+            dma((3, n)),
+            dma((3, n)),
+            dma((n,)),
+            dma((n,)),
             dma((2, n)),
             dma((2, n)),
-            dma((n,)),
-            dma((n,)),
-            dma((n,)),
-            dma((n,)),
         ],
         compiler_params=pltpu.CompilerParams(
             collective_id=0, has_side_effects=True, vmem_limit_bytes=62 << 20

time: 31.2 us -> 26.5 us (0.85)
  Pallas kernels: 29.2 us -> 25.6 us
  local copies, waits for them, and re-layouts: 1.87 us -> 0.8 us
    pallas_call x1, Pallas kernels: 29.2 us -> 25.6 us  [on_device(): pl.pallas_call(functools.partial(kernel, n, span, groups, size), name='to...]
    unnamed x1, local copies, waits for them, and re-layouts: 1.87 us -> 0.8 us
where the time goes in v2:
time: 26.5 us; the launch traced here: 26.4 us
  Pallas kernels  25.6 us (97%)
  local copies, waits for them, and re-layouts  0.8 us (3%)
    pallas_call x1, Pallas kernels, on_device(): pl.pallas_call(functools.partial(kernel, n, span, groups, size), name='to...  25.6 us
    unnamed x1, local copies, waits for them, and re-layouts  0.8 us

profile of v2, /device:TPU:16, one launch (start us, length us, event | category | flops | bytes accessed | tf_op | source)
XLA Modules:
  0.0 26.4 jit_solution(631839440061408123)
XLA Ops:
  0.0 25.6 %toeplitz_conv.1 = bf16[2048,128]{1,0:T(8,128)(2,1)S(1)} custom-call(bf16[2048,128]{1,0:T(8,128)(2,1)} %q_hbm.1, bf16[2048,128]{1,0:T(8,128)(2,1)} %k_hbm.1, bf16[2048,128]{1,0:T(8,128)(2,1)} %v_hbm.1, f32[3,128]{1,0:T(4,128)} %taps_hbm.1, f32[1,128]{1,0:T(1,128)} %bitcast.8, f32[1,32]{1,0:T(1,128)} %bitcast.9, f32[1,32]{1,0:T(1,128)} %bitcast.10, ...), custom_call_target="tpu_custom_call" | custom-call | tf_op jit(solution)/shard_map/toeplitz_conv/pallas_call | solution.py:411
  25.6 0.8 %copy.15 = bf16[2048,128]{1,0:T(8,128)(2,1)} copy(bf16[2048,128]{1,0:T(8,128)(2,1)S(1)} %toeplitz_conv.1) | data formatting | bytes 1048576

commit v3 on v2

--- a/solution.py
+++ b/solution.py
@@ -15,6 +15,7 @@
 
 TB = 256
 CHAIN = 16
+FAR = ((1, 2), (1, 1), (1, 3), (0, 2), (1, 0), (0, 1), (0, 3))
 
 PI_A = 3.140625
 PI_B = 9.67025756835938e-04
@@ -110,19 +111,24 @@
     part = blocks * rows
     pad = CHAIN * rows
 
-    def peer(j):
-        return lax.rem(me + j, n)
-
-    def source(j):
-        return lax.rem(me + (n - j), n)
+    side, place = me // 4, lax.rem(me, 4)
+
+    def peer(step):
+        return lax.rem(side + step[0], 2) * 4 + lax.rem(place + step[1], 4)
+
+    def source(step):
+        return lax.rem(side + step[0], 2) * 4 + lax.rem(place + 4 - step[1], 4)
+
+    def slot(step):
+        return step[0] * 4 + step[1]
 
     load_v = pltpu.make_async_copy(v_hbm, v_ref, in_sem.at[0])
     load_k = pltpu.make_async_copy(k_hbm, k_ref, in_sem.at[1])
     load_q = pltpu.make_async_copy(q_hbm, q_ref, in_sem.at[2])
     barrier = pltpu.get_barrier_semaphore()
-    for j in range(1, n):
+    for step in FAR:
         pl.semaphore_signal(
-            barrier, inc=1, device_id={"ctx": peer(j)}, device_id_type=MESH
+            barrier, inc=1, device_id={"ctx": peer(step)}, device_id_type=MESH
         )
     load_v.start()
     load_k.start()
@@ -156,13 +162,14 @@
         dst_ref=halo_ref,
         send_sem=halo_send,
         recv_sem=halo_recv,
-        device_id={"ctx": peer(1)},
+        device_id={"ctx": lax.rem(me + 1, n)},
         device_id_type=MESH,
     )
     halo.start()
 
     ext_ref[8:, :] = v_ref[...].astype(F32)
-    loads[0].wait()
+    for load in loads:
+        load.wait()
     load_k.wait()
     taps = taps_ref[...]
 
@@ -185,39 +192,38 @@
                 ).astype(BF16)
         return 0
 
-    lax.fori_loop(1, blocks // 2, one_pair, 0)
+    for i in range(1, blocks // 2):
+        one_pair(i, 0)
 
     parts = [(0, size, part - size), (0, 0, size), (1, 0, part)]
 
-    def x_copy(j, p):
+    def x_copy(step, p):
         h, first, count = parts[p]
         at = pl.multiple_of(pad + me * part + first, 16)
         return pltpu.make_async_remote_copy(
-            src_ref=xs_ref.at[peer(j), pl.ds(h * part + first, count), :],
+            src_ref=xs_ref.at[peer(step), pl.ds(h * part + first, count), :],
             dst_ref=xe_ref.at[h, pl.ds(at, count), :],
-            send_sem=x_send.at[p, j],
-            recv_sem=x_recv.at[p, j],
-            device_id={"ctx": peer(j)},
+            send_sem=x_send.at[p, slot(step)],
+            recv_sem=x_recv.at[p, slot(step)],
+            device_id={"ctx": peer(step)},
             device_id_type=MESH,
         )
 
-    def x_wait(j, p):
+    def x_wait(step, p):
         h, first, count = parts[p]
-        at = pl.multiple_of(pad + source(j) * part + first, 16)
+        at = pl.multiple_of(pad + source(step) * part + first, 16)
         pltpu.make_async_remote_copy(
-            src_ref=xs_ref.at[peer(j), pl.ds(h * part + first, count), :],
+            src_ref=xs_ref.at[peer(step), pl.ds(h * part + first, count), :],
             dst_ref=xe_ref.at[h, pl.ds(at, count), :],
-            send_sem=x_send.at[p, j],
-            recv_sem=x_recv.at[p, j],
-            device_id={"ctx": peer(j)},
+            send_sem=x_send.at[p, slot(step)],
+            recv_sem=x_recv.at[p, slot(step)],
+            device_id={"ctx": peer(step)},
             device_id_type=MESH,
         ).wait()
 
-    for j in range(1, n):
-        x_copy(j, 0).start()
-
-    for load in loads[1:]:
-        load.wait()
+    for step in FAR:
+        x_copy(step, 0).start()
+
     freq = column(freqs_ref[...]) * (2.0 * math.pi)
     phase = column(phases_ref[...])
     bias1 = column(b1_ref[...])
@@ -225,7 +231,7 @@
     rate = column(rates_ref[...])
     wide = span
 
-    def some_positions(i, _):
+    def some_positions(i):
         start = me * span + i * wide
         lanes = lax.broadcasted_iota(jnp.int32, (1, wide), 1) + start
         scaled = lanes.astype(F32) / seq
@@ -240,50 +246,72 @@
                 hs_ref[g, pl.ds(i * (wide // 128) + t, 1), :] = values[
                     g : g + 1, t * 128 : (t + 1) * 128
                 ]
-        return 0
-
-    lax.fori_loop(0, span // wide, some_positions, 0)
+
+    for i in range(span // wide):
+        some_positions(i)
 
     tiles = span // 128
 
-    def h_copy(j):
+    def h_copy(step):
         return pltpu.make_async_remote_copy(
-            src_ref=hs_ref.at[peer(j)],
+            src_ref=hs_ref.at[peer(step)],
             dst_ref=ha_ref.at[pl.ds(pl.multiple_of(me * tiles, 8), tiles), :],
-            send_sem=h_send.at[j],
-            recv_sem=h_recv.at[j],
-            device_id={"ctx": peer(j)},
+            send_sem=h_send.at[slot(step)],
+            recv_sem=h_recv.at[slot(step)],
+            device_id={"ctx": peer(step)},
             device_id_type=MESH,
         )
+
+    for step in FAR:
+        h_copy(step).start()
+    def h_wait(step):
+        at = pl.multiple_of(source(step) * tiles, 8)
+        pltpu.make_async_remote_copy(
+            src_ref=hs_ref.at[peer(step)],
+            dst_ref=ha_ref.at[pl.ds(at, tiles), :],
+            send_sem=h_send.at[slot(step)],
+            recv_sem=h_recv.at[slot(step)],
+            device_id={"ctx": peer(step)},
+            device_id_type=MESH,
+        ).wait()
 
     halo.wait()
     ext_ref[0:8, :] = jnp.where(me > 0, halo_ref[8:16, :].astype(F32), 0.0)
     one_pair(0, 0)
-    for j in range(1, n):
-        x_copy(j, 1).start()
-    for j in range(1, n):
-        h_copy(j).start()
-    for j in range(1, n):
-        x_copy(j, 2).start()
+    for step in FAR:
+        x_copy(step, 1).start()
+    for step in FAR:
+        x_copy(step, 2).start()
     for h in range(2):
         at = pl.multiple_of(pad + me * part, 16)
         xe_ref[h, pl.ds(at, part), :] = xs_ref[me, h * part : (h + 1) * part, :]
     ha_ref[pl.ds(pl.multiple_of(me * tiles, 8), tiles), :] = hs_ref[me]
-    for j in range(1, n):
-        h_copy(j).wait()
 
     at_row = lax.broadcasted_iota(jnp.int32, (128, 128), 0)
     at_col = lax.broadcasted_iota(jnp.int32, (128, 128), 1)
     keep = at_col >= at_row
     f_ref[0] = jnp.zeros((128, 128), BF16)
 
-    def one_tile(t, before):
-        row = jnp.broadcast_to(ha_ref[pl.ds(t, 1), :], (128, 128))
-        turned = pltpu.roll(row, 0, 1, stride=1, stride_axis=0)
-        f_ref[t + 1] = jnp.where(keep, turned, before).astype(BF16)
-        return turned
-
-    lax.fori_loop(0, seq // 128, one_tile, jnp.zeros((128, 128), F32), unroll=32)
+    def turned_row(at):
+        row = jnp.broadcast_to(ha_ref[pl.ds(at, 1), :], (128, 128))
+        return pltpu.roll(row, 0, 1, stride=1, stride_axis=0)
+
+    for step in ((0, 0),) + FAR[::-1]:
+        if step != (0, 0):
+            h_wait(step)
+        first = source(step) * tiles
+        before = turned_row(first)
+        for i in range(1, tiles):
+            here = turned_row(first + i)
+            f_ref[first + i + 1] = jnp.where(keep, here, before).astype(BF16)
+            before = here
+    for s in range(n):
+        here = turned_row(s * tiles)
+        if s == 0:
+            before = jnp.zeros((128, 128), F32)
+        else:
+            before = turned_row(s * tiles - 1)
+        f_ref[s * tiles + 1] = jnp.where(keep, here, before).astype(BF16)
 
     def lag_block(lag):
         low, mid, high = f_ref[2 * lag], f_ref[2 * lag + 1], f_ref[2 * lag + 2]
@@ -291,72 +319,88 @@
             [jnp.concatenate([mid, high], 1), jnp.concatenate([low, mid], 1)], 0
         )
 
-    def y_copy(h, to):
-        j = lax.rem(to - me + n, n)
+    halves = [(0, part), (part, part), (0, 2 * part)]
+
+    def y_copy(kind, to, other, index):
+        first, count = halves[kind]
         return pltpu.make_async_remote_copy(
-            src_ref=ys_ref.at[h, to],
-            dst_ref=yr_ref.at[h, me],
-            send_sem=y_send.at[h, j],
-            recv_sem=y_recv.at[h, j],
+            src_ref=ys_ref.at[to, pl.ds(first, count), :],
+            dst_ref=yr_ref.at[other, pl.ds(first, count), :],
+            send_sem=y_send.at[kind, index],
+            recv_sem=y_recv.at[kind, index],
             device_id={"ctx": to},
             device_id_type=MESH,
         )
 
-    pairs = n // 2
-    wide_rows = 2 * part
+    def shifted(h, start, count):
+        if start % 16 == 0:
+            return xe_ref[h, start : start + count, :]
+        return xo_ref[h, start + rows : start + rows + count, :]
+
+    def chain(halves_of, first, count, lags):
+        left = [
+            jnp.concatenate(
+                [shifted(h, pad + first - lag * rows, count) for h in halves_of], 0
+            )
+            for lag in range(lags)
+        ]
+        right = [lag_block(lag) for lag in range(lags)]
+        return jnp.dot(
+            jnp.concatenate(left, 1),
+            jnp.concatenate(right, 0),
+            preferred_element_type=F32,
+        ).astype(BF16)
+
     for h in range(2):
         for p in range(3):
             if parts[p][0] == h:
-                for j in range(1, n):
-                    x_wait(j, p)
+                for step in FAR[::-1]:
+                    x_wait(step, p)
         whole = xe_ref[h].astype(F32)
         xo_ref[h] = jnp.concatenate(
             [jnp.zeros((rows, TB), F32), whole[: whole.shape[0] - rows]], 0
         ).astype(BF16)
 
-        def one_pair_of_spans(k, _, h=h):
-            two = lax.rem(me // 2 + 1 + k, pairs)
-            for c in range(pairs):
-
-                @pl.when(two == c)
-                def _(c=c):
-                    left, right = [], []
-                    for lag in range((c + 1) * CHAIN):
-                        start = pad + c * wide_rows - lag * rows
-                        if start % 16 == 0:
-                            left.append(xe_ref[h, start : start + wide_rows, :])
-                        else:
-                            start = start + rows
-                            left.append(xo_ref[h, start : start + wide_rows, :])
-                        right.append(lag_block(lag))
-                    out = jnp.dot(
-                        jnp.concatenate(left, 1),
-                        jnp.concatenate(right, 0),
-                        preferred_element_type=F32,
-                    ).astype(BF16)
-                    ys_ref[h, 2 * c] = out[:part]
-                    ys_ref[h, 2 * c + 1] = out[part:]
-
-            @pl.when(k < pairs - 1)
-            def _():
-                y_copy(h, 2 * two).start()
-                y_copy(h, 2 * two + 1).start()
-
-            return 0
-
-        lax.fori_loop(0, pairs, one_pair_of_spans, 0)
-        y_copy(h, me + 1 - 2 * lax.rem(me, 2)).start()
-        yr_ref[h, me] = ys_ref[h, me]
+        for other in range(2):
+
+            @pl.when(side == 1 - other)
+            def _(other=other, h=h):
+                for c in (4 * other + 2, 4 * other):
+                    out = chain((h,), c * part, 2 * part, (c + 2) * blocks)
+                    ys_ref[c, h * part : (h + 1) * part] = out[:part]
+                    ys_ref[c + 1, h * part : (h + 1) * part] = out[part:]
+
+        for move in (2, 1, 3, 0):
+            y_copy(h, peer((1, move)), me, move).start()
+
+    def one_span(i, _):
+        move = (1 - i // 2) * (2 + i) + (i // 2) * (3 - i)
+        to = side * 4 + lax.rem(place + move, 4)
+        for c in range(n):
+
+            @pl.when(to == c)
+            def _(c=c):
+                ys_ref[c] = chain((0, 1), c * part, part, (c + 1) * blocks)
+
+        @pl.when(i < 3)
+        def _():
+            y_copy(2, to, me, move).start()
+
+        return 0
+
+    lax.fori_loop(0, 4, one_span, 0)
+    yr_ref[me] = ys_ref[me]
 
     load_q.wait()
-    for h in range(2):
-        for j in range(1, n):
+    for step in FAR:
+        for kind in (0, 1) if step[0] else (2,):
+            first, count = halves[kind]
             pltpu.make_async_remote_copy(
-                src_ref=ys_ref.at[h, peer(j)],
-                dst_ref=yr_ref.at[h, source(j)],
-                send_sem=y_send.at[h, j],
-                recv_sem=y_recv.at[h, j],
-                device_id={"ctx": peer(j)},
+                src_ref=ys_ref.at[peer(step), pl.ds(first, count), :],
+                dst_ref=yr_ref.at[source(step), pl.ds(first, count), :],
+                send_sem=y_send.at[kind, step[1]],
+                recv_sem=y_recv.at[kind, step[1]],
+                device_id={"ctx": peer(step)},
                 device_id_type=MESH,
             ).wait()
 
@@ -365,7 +409,7 @@
     def last_pair(i, _):
         row = pl.multiple_of(i * size, size)
         two = [
-            yr_ref[h, g, pl.ds(row, size), :].astype(F32)
+            yr_ref[g, pl.ds(pl.multiple_of(h * part + row, 16), size), :].astype(F32)
             for g in range(groups)
             for h in range(2)
         ]
@@ -437,8 +481,8 @@
             pltpu.VMEM((groups, span // 128, 128), F32),
             pltpu.VMEM((seq // 128, 128), F32),
             pltpu.VMEM((seq // 128 + 1, 128, 128), BF16),
-            pltpu.VMEM((2, n, part, TB), BF16),
-            pltpu.VMEM((2, groups, part, TB), BF16),
+            pltpu.VMEM((n, piece, TB), BF16),
+            pltpu.VMEM((groups, piece, TB), BF16),
             dma((3,)),
             dma((10,)),
             dma,
@@ -447,8 +491,8 @@
             dma((3, n)),
             dma((n,)),
             dma((n,)),
-            dma((2, n)),
-            dma((2, n)),
+            dma((3, 4)),
+            dma((3, 4)),
         ],
         compiler_params=pltpu.CompilerParams(
             collective_id=0, has_side_effects=True, vmem_limit_bytes=62 << 20

time: 26.5 us -> 25 us (0.943)
  Pallas kernels: 25.6 us -> 24.1 us
    pallas_call x1, Pallas kernels: 25.6 us -> 24.1 us  [on_device(): pl.pallas_call(functools.partial(kernel, n, span, groups, size), name='to...]
where the time goes in v3:
time: 25 us; the launch traced here: 24.9 us
  Pallas kernels  24.1 us (96%)
  local copies, waits for them, and re-layouts  0.8 us (3%)
    pallas_call x1, Pallas kernels, on_device(): pl.pallas_call(functools.partial(kernel, n, span, groups, size), name='to...  24.1 us
    unnamed x1, local copies, waits for them, and re-layouts  0.8 us

profile of v3, /device:TPU:16, one launch (start us, length us, event | category | flops | bytes accessed | tf_op | source)
XLA Modules:
  0.0 24.9 jit_solution(16437463413322056602)
XLA Ops:
  0.0 24.1 %toeplitz_conv.1 = bf16[2048,128]{1,0:T(8,128)(2,1)S(1)} custom-call(bf16[2048,128]{1,0:T(8,128)(2,1)} %q_hbm.1, bf16[2048,128]{1,0:T(8,128)(2,1)} %k_hbm.1, bf16[2048,128]{1,0:T(8,128)(2,1)} %v_hbm.1, f32[3,128]{1,0:T(4,128)} %taps_hbm.1, f32[1,128]{1,0:T(1,128)} %bitcast.8, f32[1,32]{1,0:T(1,128)} %bitcast.9, f32[1,32]{1,0:T(1,128)} %bitcast.10, ...), custom_call_target="tpu_custom_call" | custom-call | tf_op jit(solution)/shard_map/toeplitz_conv/pallas_call | solution.py:455
  24.1 0.8 %copy.15 = bf16[2048,128]{1,0:T(8,128)(2,1)} copy(bf16[2048,128]{1,0:T(8,128)(2,1)S(1)} %toeplitz_conv.1) | data formatting | bytes 1048576

commit v4 on v3

--- a/solution.py
+++ b/solution.py
@@ -11,29 +11,31 @@
 MESH = pl.DeviceIdType.MESH
 F32 = jnp.float32
 BF16 = jnp.bfloat16
-HIGHEST = lax.Precision.HIGHEST
 
 TB = 256
 CHAIN = 16
 FAR = ((1, 2), (1, 1), (1, 3), (0, 2), (1, 0), (0, 1), (0, 3))
 
-PI_A = 3.140625
-PI_B = 9.67025756835938e-04
-PI_C = 6.277114152908325e-07
-
-
-def sine(x):
-    turns = jnp.floor(x * (1.0 / math.pi) + 0.5)
-    r = ((x - turns * PI_A) - turns * PI_B) - turns * PI_C
-    odd = turns - 2.0 * jnp.floor(turns * 0.5)
-    r = r * (1.0 - 2.0 * odd)
+TURN_A = 6.28125
+TURN_B = 0.001934051513671875
+TURN_C = 1.2556658930407139e-06
+TURN_BC = 0.0019353071693331003
+
+
+def sine(x, small=False):
+    turns = jnp.round(x * (0.5 / math.pi))
+    r = x - turns * TURN_A
+    if small:
+        r = r - turns * TURN_BC
+    else:
+        r = (r - turns * TURN_B) - turns * TURN_C
     r2 = r * r
-    tail = -2.5052108e-8 + r2 * 1.6059044e-10
-    tail = 2.7557319e-6 + r2 * tail
-    tail = -1.9841270e-4 + r2 * tail
-    tail = 8.3333333e-3 + r2 * tail
-    tail = -1.6666667e-1 + r2 * tail
-    return r + r * r2 * tail
+    tail = -2.4676328536088477e-08 + r2 * 1.3449288904787693e-10
+    tail = 2.7529381441127043e-06 + r2 * tail
+    tail = -0.00019840151071548462 + r2 * tail
+    tail = 0.00833331048488617 + r2 * tail
+    tail = -0.166666641831398 + r2 * tail
+    return r + r * (r2 * tail)
 
 
 def column(row):
@@ -44,9 +46,20 @@
     return jnp.sum(jnp.where(at_row == at_col, square, 0.0), axis=1, keepdims=True)
 
 
-def rows_to_rows(a, b):
-    return lax.dot_general(
-        a, b, (((0,), (0,)), ((), ())), precision=HIGHEST, preferred_element_type=F32
+def high_low(value):
+    high = value.astype(BF16)
+    return high, (value - high.astype(F32)).astype(BF16)
+
+
+def stacked(weights):
+    high, low = high_low(weights)
+    return jnp.concatenate([high, high, low], 1)
+
+
+def product(stack, value):
+    high, low = high_low(value)
+    return jnp.dot(
+        stack, jnp.concatenate([high, low, high], 0), preferred_element_type=F32
     )
 
 
@@ -229,6 +242,10 @@
     bias1 = column(b1_ref[...])
     bias2 = column(b2_ref[...])
     rate = column(rates_ref[...])
+    layer1 = stacked(w1_ref[...].T)
+    layer2 = stacked(w2_ref[...].T)
+    layer3 = stacked(wo_ref[...])
+
     wide = span
 
     def some_positions(i):
@@ -236,11 +253,9 @@
         lanes = lax.broadcasted_iota(jnp.int32, (1, wide), 1) + start
         scaled = lanes.astype(F32) / seq
         feature = sine(freq * scaled + phase)
-        first = sine(rows_to_rows(w1_ref[...], feature) + bias1)
-        second = sine(rows_to_rows(w2_ref[...], first) + bias2)
-        values = lax.dot(
-            wo_ref[...], second, precision=HIGHEST, preferred_element_type=F32
-        ) * jnp.exp(-rate * scaled)
+        first = sine(product(layer1, feature) + bias1, small=True)
+        second = sine(product(layer2, first) + bias2, small=True)
+        values = product(layer3, second) * jnp.exp(-rate * scaled)
         for t in range(wide // 128):
             for g in range(groups):
                 hs_ref[g, pl.ds(i * (wide // 128) + t, 1), :] = values[
@@ -422,7 +437,8 @@
             ).astype(BF16)
         return 0
 
-    lax.fori_loop(0, blocks // 2, last_pair, 0)
+    for i in range(blocks // 2):
+        last_pair(i, 0)
 
 
 def on_device(

time: 25 us -> 24.9 us (level)
  no operation moved by 1% of the time
where the time goes in v4:
time: 24.9 us; the launch traced here: 24.8 us
  Pallas kernels  24 us (96%)
  local copies, waits for them, and re-layouts  0.8 us (3%)
    pallas_call x1, Pallas kernels, on_device(): pl.pallas_call(functools.partial(kernel, n, span, groups, size), name='to...  24 us
    unnamed x1, local copies, waits for them, and re-layouts  0.8 us

profile of v4, /device:TPU:16, one launch (start us, length us, event | category | flops | bytes accessed | tf_op | source)
XLA Modules:
  0.0 24.8 jit_solution(14496473594656595778)
XLA Ops:
  0.0 24.0 %toeplitz_conv.1 = bf16[2048,128]{1,0:T(8,128)(2,1)S(1)} custom-call(bf16[2048,128]{1,0:T(8,128)(2,1)} %q_hbm.1, bf16[2048,128]{1,0:T(8,128)(2,1)} %k_hbm.1, bf16[2048,128]{1,0:T(8,128)(2,1)} %v_hbm.1, f32[3,128]{1,0:T(4,128)} %taps_hbm.1, f32[1,128]{1,0:T(1,128)} %bitcast.8, f32[1,32]{1,0:T(1,128)} %bitcast.9, f32[1,32]{1,0:T(1,128)} %bitcast.10, ...), custom_call_target="tpu_custom_call" | custom-call | tf_op jit(solution)/shard_map/toeplitz_conv/pallas_call | solution.py:471
  24.0 0.8 %copy.15 = bf16[2048,128]{1,0:T(8,128)(2,1)} copy(bf16[2048,128]{1,0:T(8,128)(2,1)S(1)} %toeplitz_conv.1) | data formatting | bytes 1048576

commit v5 on v4

--- a/solution.py
+++ b/solution.py
@@ -371,10 +371,9 @@
             if parts[p][0] == h:
                 for step in FAR[::-1]:
                     x_wait(step, p)
-        whole = xe_ref[h].astype(F32)
-        xo_ref[h] = jnp.concatenate(
-            [jnp.zeros((rows, TB), F32), whole[: whole.shape[0] - rows]], 0
-        ).astype(BF16)
+        count = pad + n * part
+        xo_ref[h, 0:rows, :] = jnp.zeros((rows, TB), BF16)
+        xo_ref[h, rows:count, :] = xe_ref[h, 0 : count - rows, :]
 
         for other in range(2):
 
@@ -391,7 +390,7 @@
     def one_span(i, _):
         move = (1 - i // 2) * (2 + i) + (i // 2) * (3 - i)
         to = side * 4 + lax.rem(place + move, 4)
-        for c in range(n):
+        for c in range(n // 2, n):
 
             @pl.when(to == c)
             def _(c=c):
@@ -403,7 +402,17 @@
 
         return 0
 
-    lax.fori_loop(0, 4, one_span, 0)
+    @pl.when(side == 0)
+    def _():
+        for c in range(n // 2):
+            ys_ref[c] = chain((0, 1), c * part, part, (c + 1) * blocks)
+        for move in (2, 3, 1):
+            y_copy(2, peer((0, move)), me, move).start()
+
+    @pl.when(side == 1)
+    def _():
+        lax.fori_loop(0, 4, one_span, 0)
+
     yr_ref[me] = ys_ref[me]
 
     load_q.wait()

time: 24.9 us -> 24.7 us (level)
  no operation moved by 1% of the time
where the time goes in v5:
time: 24.7 us; the launch traced here: 24.6 us
  Pallas kernels  23.8 us (96%)
  local copies, waits for them, and re-layouts  0.8 us (3%)
    pallas_call x1, Pallas kernels, on_device(): pl.pallas_call(functools.partial(kernel, n, span, groups, size), name='to...  23.8 us
    unnamed x1, local copies, waits for them, and re-layouts  0.8 us

profile of v5, /device:TPU:16, one launch (start us, length us, event | category | flops | bytes accessed | tf_op | source)
XLA Modules:
  0.0 24.6 jit_solution(1398852712248392272)
XLA Ops:
  0.0 23.8 %toeplitz_conv.1 = bf16[2048,128]{1,0:T(8,128)(2,1)S(1)} custom-call(bf16[2048,128]{1,0:T(8,128)(2,1)} %q_hbm.1, bf16[2048,128]{1,0:T(8,128)(2,1)} %k_hbm.1, bf16[2048,128]{1,0:T(8,128)(2,1)} %v_hbm.1, f32[3,128]{1,0:T(4,128)} %taps_hbm.1, f32[1,128]{1,0:T(1,128)} %bitcast.8, f32[1,32]{1,0:T(1,128)} %bitcast.9, f32[1,32]{1,0:T(1,128)} %bitcast.10, ...), custom_call_target="tpu_custom_call" | custom-call | tf_op jit(solution)/shard_map/toeplitz_conv/pallas_call | solution.py:480
  23.8 0.8 %copy.15 = bf16[2048,128]{1,0:T(8,128)(2,1)} copy(bf16[2048,128]{1,0:T(8,128)(2,1)S(1)} %toeplitz_conv.1) | data formatting | bytes 1048576

commit v6 on v5

--- a/solution.py
+++ b/solution.py
@@ -14,7 +14,7 @@
 
 TB = 256
 CHAIN = 16
-FAR = ((1, 2), (1, 1), (1, 3), (0, 2), (1, 0), (0, 1), (0, 3))
+FAR = ((1, 2), (1, 1), (1, 3), (1, 0), (0, 2), (0, 1), (0, 3))
 
 TURN_A = 6.28125
 TURN_B = 0.001934051513671875

time: 24.7 us -> 24.8 us (level)
  no operation moved by 1% of the time
where the time goes in v6:
time: 24.8 us; the launch traced here: 24.7 us
  Pallas kernels  23.9 us (96%)
  local copies, waits for them, and re-layouts  0.8 us (3%)
    pallas_call x1, Pallas kernels, on_device(): pl.pallas_call(functools.partial(kernel, n, span, groups, size), name='to...  23.9 us
    unnamed x1, local copies, waits for them, and re-layouts  0.8 us

profile of v6, /device:TPU:16, one launch (start us, length us, event | category | flops | bytes accessed | tf_op | source)
XLA Modules:
  0.0 24.7 jit_solution(11099470083474396787)
XLA Ops:
  0.0 23.9 %toeplitz_conv.1 = bf16[2048,128]{1,0:T(8,128)(2,1)S(1)} custom-call(bf16[2048,128]{1,0:T(8,128)(2,1)} %q_hbm.1, bf16[2048,128]{1,0:T(8,128)(2,1)} %k_hbm.1, bf16[2048,128]{1,0:T(8,128)(2,1)} %v_hbm.1, f32[3,128]{1,0:T(4,128)} %taps_hbm.1, f32[1,128]{1,0:T(1,128)} %bitcast.8, f32[1,32]{1,0:T(1,128)} %bitcast.9, f32[1,32]{1,0:T(1,128)} %bitcast.10, ...), custom_call_target="tpu_custom_call" | custom-call | tf_op jit(solution)/shard_map/toeplitz_conv/pallas_call | solution.py:480
  23.9 0.8 %copy.15 = bf16[2048,128]{1,0:T(8,128)(2,1)} copy(bf16[2048,128]{1,0:T(8,128)(2,1)S(1)} %toeplitz_conv.1) | data formatting | bytes 1048576
